TPU v7x, 32 devices: a whole 2x2x4 slice. The times are simulated.
32 devices in a mesh: grp: 4 (over y, x), dev: 8 (over z, core).
Axes of the slice: x: 2, y: 2, z: 4, core: 2. Of those that a mesh axis runs over, the one named last changes fastest.
Arguments:
- functions: bfloat16 [6144, 3072], P('dev', 'grp'), may hold values from -6 to 6
- applied: bfloat16 [6144, 3072], P('dev', 'grp'), may hold values from -6 to 6
- kernel: bfloat16 [6144, 768], P('dev'), may hold values from -0.21875 to 0.21875
- live_counts: int32 [8, 8], P('dev'), may hold values from 24 to 96, as said below
- coef_counts: int32 [4, 8], P('grp', 'dev'), may hold values from 192 to 768, as said below
Outputs:
- gradient: bfloat16 [6144, 3072], P('dev', 'grp')
Inputs may be any that keep to these rules, and one draw needn't show every extreme that they name: `live_counts`: no owner fills more than 96 slots of a neighborhood; some neighborhood gets 96 live slots from every owner, and some entry is the smallest value. `coef_counts`: some region has all 768 coefficients live, and some has the smallest count.
All inputs are finite; a program needn't handle non-finite values.
Results may differ from a plain program's by a relative error of at most 0.017.
Values may be sent and summed in bfloat16 or wider, within the bound.
A program may use at most 64 MiB of HBM per device.

v0:
```python
import jax
import jax.numpy as jnp
from jax import lax
from jax.sharding import PartitionSpec as P


def shards(functions, applied, kernel, live_counts, coef_counts):
    slot_count, coef_width = functions.shape
    owners = lax.axis_size("dev")
    per_owner = slot_count // owners
    got_funcs, got_applied = (
        lax.all_to_all(functions, "dev", split_axis=0, concat_axis=0, tiled=True),
        lax.all_to_all(applied, "dev", split_axis=0, concat_axis=0, tiled=True),
    )
    slot_index = jnp.arange(slot_count, dtype=jnp.int32)
    owner_match = (slot_index // per_owner)[:, None] == jnp.arange(owners, dtype=jnp.int32)[None, :]
    limits = jnp.sum(jnp.where(owner_match, live_counts[0][None, :], 0), axis=1)
    slot_live = slot_index % per_owner < limits
    coef_live = jnp.arange(coef_width, dtype=jnp.int32) < coef_counts[0, 0]
    live_mask = slot_live[:, None] & coef_live[None, :]
    zero_value = jnp.zeros((), jnp.bfloat16)
    masked_funcs = jnp.where(live_mask, got_funcs, zero_value)
    masked_applied = jnp.where(live_mask, got_applied, zero_value)
    partial_value = lax.dot_general(
        masked_funcs, masked_applied, (((1,), (1,)), ((), ())), preferred_element_type=jnp.float32
    )
    symmetric = 0.5 * (partial_value + partial_value.T)
    kernel_part = jnp.dot(kernel, masked_applied, preferred_element_type=jnp.float32)
    tile_rows = lax.psum_scatter(
        symmetric.astype(jnp.bfloat16), "grp", scatter_dimension=0, tiled=True
    ).astype(jnp.float32)
    ham_rows = (tile_rows / coef_width).astype(jnp.bfloat16)
    columns = lax.dot_general(
        kernel, ham_rows, (((1,), (1,)), ((), ())), preferred_element_type=jnp.float32
    ).astype(jnp.bfloat16)
    multiplier_part = jnp.dot(
        lax.all_gather(columns, "grp", axis=1, tiled=True),
        masked_funcs,
        preferred_element_type=jnp.float32,
    )
    gradient = jnp.where(live_mask, kernel_part - multiplier_part, jnp.float32(0.0)).astype(
        jnp.bfloat16
    )
    return lax.all_to_all(gradient, "dev", split_axis=0, concat_axis=0, tiled=True)


def solution(mesh):
    placed = (P("dev", "grp"), P("dev", "grp"), P("dev", None), P("dev", None), P("grp", "dev"))
    return jax.shard_map(
        shards, mesh=mesh, in_specs=placed, out_specs=P("dev", "grp"), check_vma=False
    )
```

profile of v0, /device:TPU:9, one launch (start us, length us, event | category | flops | bytes accessed | tf_op | source)
XLA Modules:
  0.0 182.9 jit_solution(3210415233107061929)
XLA Ops:
  6.5 0.0 copy-start
  6.5 32.8 %all_to_all.36 = bf16[8,96,768]{2,1,0:T(8,128)(2,1)S(1)} all-to-all(bf16[8,96,768]{2,1,0:T(8,128)(2,1)} %bitcast.31), channel_id=1, replica_groups=mesh['grp'=4,'dev'=8] {'dev'}, dimensions={0} | all-to-all | bytes 2359296 | tf_op jit(solution)/shard_map/all_to_all | solution.py:12
  39.4 0.0 copy-start.3
  39.4 0.0 copy-start.5
  39.4 5.9 %all-to-all-start = ((bf16[8,96,768]{2,1,0:T(8,128)(2,1)}), bf16[8,96,768]{2,1,0:T(8,128)(2,1)S(1)}, u32[]{:S(2)}, u32[]{:S(2)}) async-start(bf16[8,96,768]{2,1,0:T(8,128)(2,1)} %bitcast.32), calls=%async_computation | async-start | bytes 2359296 | tf_op jit(solution)/shard_map/all_to_all | solution.py:13
  45.3 0.0 reduce-scatter.2.cloned.1.call-start
  45.9 0.0 copy-done.5
  45.9 0.1 select_reduce_fusion
  46.0 0.1 reduce_sum.12
  46.1 25.0 %all-to-all-done = bf16[8,96,768]{2,1,0:T(8,128)(2,1)S(1)} async-done(((bf16[8,96,768]{2,1,0:T(8,128)(2,1)}), bf16[8,96,768]{2,1,0:T(8,128)(2,1)S(1)}, u32[]{:S(2)}, u32[]{:S(2)}) %all-to-all-start) | async-done | bytes 1179680 | tf_op jit(solution)/shard_map/all_to_all | solution.py:13
  71.1 0.0 copy-done.3
  71.1 0.0 copy-start.1
  71.1 0.6 and_select_fusion.3
  71.7 0.4 copy-done.1
  72.2 1.1 fusion.25
  73.3 2.0 %copy.7 = f32[768,768]{0,1:T(8,128)} copy(f32[768,768]{1,0:T(8,128)S(1)} %fusion.25) | data formatting | bytes 4718592 | tf_op jit(solution)/shard_map/dot_general | solution.py:24
  75.3 3.0 %fusion.2 = bf16[768,768]{1,0:T(8,128)(2,1)} fusion(f32[768,768]{1,0:T(8,128)S(1)} %fusion.25, f32[768,768]{0,1:T(8,128)} %copy.7), kind=kLoop, calls=%fused_computation.8 | loop fusion | flops 1769472 | bytes 5898240 | tf_op jit(solution)/shard_map/convert_element_type | solution.py:30
  78.2 0.0 reduce-scatter.2.cloned.1.call-update
  78.3 0.0 copy-start.4
  78.3 0.0 all-gather.2.cloned.1.call-start
  78.3 30.3 %reduce-scatter.2.cloned.1.call-done = bf16[192,768]{1,0:T(8,128)(2,1)} async-done(((bf16[768,768]{1,0:T(8,128)(2,1)}), bf16[192,768]{1,0:T(8,128)(2,1)}) %reduce-scatter.2.cloned.1.call-update) | async-done | bytes 294928 | tf_op jit(solution)/shard_map/reduce_scatter | solution.py:29
  108.6 0.0 copy-done
  108.6 2.2 %fusion.8 = bf16[768,192]{0,1:T(8,128)(2,1)} fusion(bf16[768,768]{1,0:T(8,128)(2,1)S(1)} %copy-done, bf16[192,768]{1,0:T(8,128)(2,1)} %reduce-scatter.2.cloned.1.call-done), kind=kOutput, calls=%fused_computation.16 | convolution fusion | flops 227082240 | bytes 1769472 | tf_op jit(solution)/shard_map/dot_general | solution.py:33
  110.8 0.0 all-gather.2.cloned.1.call-update
  110.9 27.7 %all-gather.2.cloned.1.call-done = bf16[768,768]{0,1:T(8,128)(2,1)} async-done(((bf16[768,192]{0,1:T(8,128)(2,1)}), bf16[768,768]{0,1:T(8,128)(2,1)}) %all-gather.2.cloned.1.call-update) | async-done | bytes 1179664 | tf_op jit(solution)/shard_map/all_gather | solution.py:37
  138.6 0.0 copy-done.4
  138.6 0.0 copy-start.2
  138.6 2.6 %fusion.3 = f32[768,768]{1,0:T(8,128)S(1)} fusion(bf16[768,768]{0,1:T(8,128)(2,1)} %all-gather.2.cloned.1.call-done, bf16[768,768]{1,0:T(8,128)(2,1)S(1)} %bitcast.30, pred[768]{0:T(1024)(128)(4,1)S(1)} %iota_compare_fusion.1, pred[768]{0:T(1024)(128)(4,1)S(1)} %fusion.12), kind=kOutput, calls=%fused_computation.11 | convolution fusion | flops 907149312 | bytes 4720128 | tf_op jit(solution)/shard_map/dot_general | solution.py:36
  141.2 0.0 copy-done.2
  141.2 1.3 fusion
  142.5 32.5 %all_to_all.37 = bf16[8,96,768]{2,1,0:T(8,128)(2,1)S(1)} all-to-all(bf16[8,96,768]{2,1,0:T(8,128)(2,1)S(1)} %bitcast.33), channel_id=1, replica_groups=mesh['grp'=4,'dev'=8] {'dev'}, dimensions={0} | all-to-all | bytes 2359296 | tf_op jit(solution)/shard_map/all_to_all | solution.py:44
  175.0 1.0 copy.10
  (4 shorter events, 0.0 us)
Async XLA Ops:
  6.5 102.1 %copy-start = (bf16[768,768]{1,0:T(8,128)(2,1)S(1)}, bf16[768,768]{1,0:T(8,128)(2,1)}, u32[]{:S(2)}) copy-start(bf16[768,768]{1,0:T(8,128)(2,1)} %param.7) | copy-start | bytes 3538948
  39.4 31.8 %copy-start.3 = (bf16[8,96,768]{2,1,0:T(8,128)(2,1)}, bf16[8,96,768]{2,1,0:T(8,128)(2,1)S(1)}, u32[]{:S(2)}) copy-start(bf16[8,96,768]{2,1,0:T(8,128)(2,1)S(1)} %all_to_all.36) | copy-start | bytes 3538948
  39.4 6.6 %copy-start.5 = (s32[1,8]{1,0:T(1,128)S(1)}, s32[1,8]{1,0:T(1,128)}, u32[]{:S(2)}) copy-start(s32[1,8]{1,0:T(1,128)} %param.8) | copy-start | bytes 100
  39.4 31.8 %all-to-all-start = ((bf16[8,96,768]{2,1,0:T(8,128)(2,1)}), bf16[8,96,768]{2,1,0:T(8,128)(2,1)S(1)}, u32[]{:S(2)}, u32[]{:S(2)}) async-start(bf16[8,96,768]{2,1,0:T(8,128)(2,1)} %bitcast.32), calls=%async_computation | async-start | bytes 2359296 | tf_op jit(solution)/shard_map/all_to_all | solution.py:13
  45.3 63.3 %reduce-scatter.2.cloned.1.call-start = ((), (), s32[]{:S(2)}) async-start(), calls=%async_computation.4 | async-start | bytes 1474560 | tf_op jit(solution)/shard_map/reduce_scatter | solution.py:29
  71.1 1.0 copy-start.1
  78.3 60.3 %copy-start.4 = (bf16[8,96,768]{2,1,0:T(8,128)(2,1)S(1)}, bf16[8,96,768]{2,1,0:T(8,128)(2,1)}, u32[]{:S(2)}) copy-start(bf16[8,96,768]{2,1,0:T(8,128)(2,1)} %copy-done.3) | copy-start | bytes 3538948
  78.3 60.3 %all-gather.2.cloned.1.call-start = ((), (), s32[]{:S(2)}) async-start(), calls=%async_computation.5 | async-start | bytes 1474560 | tf_op jit(solution)/shard_map/all_gather | solution.py:37
  138.6 2.6 %copy-start.2 = (bf16[8,96,768]{2,1,0:T(8,128)(2,1)S(1)}, bf16[8,96,768]{2,1,0:T(8,128)(2,1)}, u32[]{:S(2)}) copy-start(bf16[8,96,768]{2,1,0:T(8,128)(2,1)} %copy-done.1) | copy-start | bytes 3538948
Sparse Core Ops, SparseCore 0:
  78.4 30.1 reduce-scatter.1
  111.0 27.5 all-gather.1
where the time goes:
time: 186 us; the launch traced here: 183 us
  waiting for transfers between devices  83 us (45%)
  blocking collectives  65.3 us (35%)
  between operations  14.1 us (8%)
  matrix products  7.28 us (4%)
  starting transfers between devices  5.94 us (3%)
  other arithmetic  3.72 us (2%)
  local copies, waits for them, and re-layouts  3.49 us (2%)
    all_to_all x1, blocking collectives, shards(): lax.all_to_all(functions, 'dev', split_axis=0, concat_axis=0, tiled=True)  32.8 us
    all_to_all x1, blocking collectives, shards(): lax.all_to_all(gradient, 'dev', split_axis=0, concat_axis=0, tiled=True)  32.5 us
    reduce_scatter x1, waiting for transfers between devices, shards(): lax.psum_scatter(symmetric.astype(jnp.bfloat16), 'grp', scatter_dimension...  30.3 us
    all_gather x1, waiting for transfers between devices, shards(): lax.all_gather(columns, 'grp', axis=1, tiled=True)  27.7 us
    all_to_all x1, waiting for transfers between devices, shards(): lax.all_to_all(applied, 'dev', split_axis=0, concat_axis=0, tiled=True)  25 us
    all_to_all x1, starting transfers between devices, shards(): lax.all_to_all(applied, 'dev', split_axis=0, concat_axis=0, tiled=True)  5.9 us
  transfers between devices with their start and end apart: 3, of which 3 were waited for; matrix products, arithmetic and copies ran while one was open for 0% of the time, Pallas kernels for 0%

commit v1 on v0

v1 whole, which is shorter than its diff:
```python
import functools

import jax
import jax.numpy as jnp
from jax import lax
from jax.experimental import pallas as pl
from jax.experimental.pallas import tpu as pltpu
from jax.sharding import PartitionSpec as P

MESH = pl.DeviceIdType.MESH
CORES = 2
BANDS = 8


def arrival_orders(chips):
    half = chips // 2
    return [
        sorted(range(chips), key=lambda s: (abs(s - z), (s < half) != (z < half), s)) for z in range(chips)
    ]


def pick(index, values):
    if all(v == values[0] for v in values):
        return values[0]
    found = jnp.int32(values[0])
    for k in range(1, len(values)):
        found = jnp.where(index == k, jnp.int32(values[k]), found)
    return found


def body(
    n_grp, n_dev, live_ref, coef_ref, f_hbm, a_hbm, k_hbm, out_ref,
    land_f, land_a, land_k, fm, am, kp, ka, s_loc, s_in, low, ham, g_buf,
    f_send, f_recv, a_send, a_recv, s_send, s_recv, g_send, g_recv, k_sem, own_sem,
):
    per, coef = f_hbm.shape[1:]
    slots = n_dev * per
    chips = n_dev // CORES
    bands = min(BANDS, n_dev)
    group = n_dev // bands
    rows = group * per
    grp, dev = lax.axis_index("grp"), lax.axis_index("dev")
    chip, core = dev // CORES, dev % CORES
    other = 1 - core
    orders = arrival_orders(chips)

    sources = []
    for p in range(chips):
        z = pick(chip, [orders[k][p] for k in range(chips)])
        sources += [z * CORES + core, z * CORES + other]
    sends = []
    for p in range(1, chips):
        z = pick(chip, [orders[k][p] for k in range(chips)])
        spot = pick(chip, [orders[orders[k][p]].index(k) for k in range(chips)])
        sends += [(z * CORES + core, spot * CORES), (z * CORES + other, spot * CORES + 1)]
    sends.append((chip * CORES + other, 1))

    k_copies = [
        pltpu.make_async_copy(k_hbm.at[sources[i]], land_k.at[i], k_sem.at[i]) for i in range(n_dev)
    ]
    own = [
        pltpu.make_async_copy(f_hbm.at[dev], land_f.at[0], own_sem.at[0]),
        pltpu.make_async_copy(a_hbm.at[dev], land_a.at[0], own_sem.at[1]),
    ]

    barrier = pltpu.get_barrier_semaphore()
    for r in range(1, n_dev):
        pl.semaphore_signal(barrier, inc=1, device_id={"dev": (dev + r) % n_dev}, device_id_type=MESH)
    for r in range(1, n_grp):
        pl.semaphore_signal(barrier, inc=1, device_id={"grp": (grp + r) % n_grp}, device_id_type=MESH)
    for copy in own + k_copies:
        copy.start()
    pl.semaphore_wait(barrier, n_dev + n_grp - 2)

    outgoing = []
    for number, (target, spot) in enumerate(sends):
        for src, dst, ss, rs in ((f_hbm, land_f, f_send, f_recv), (a_hbm, land_a, a_send, a_recv)):
            copy = pltpu.make_async_remote_copy(
                src_ref=src.at[target], dst_ref=dst.at[spot],
                send_sem=ss.at[number], recv_sem=rs.at[spot],
                device_id={"dev": target}, device_id_type=MESH,
            )
            copy.start()
            outgoing.append(copy)

    def flat(ref, band):
        pieces = [ref[band * group + t].astype(jnp.float32) for t in range(group)]
        return jnp.concatenate(pieces, axis=0) if group > 1 else pieces[0]

    def band_slice(band):
        return pl.ds(band * rows, rows)

    column = lax.broadcasted_iota(jnp.int32, (1, slots), 1)
    target_row = jnp.zeros((1, slots), jnp.int32)
    for i in range(n_dev):
        inside = (column >= i * per) & (column < (i + 1) * per)
        target_row = jnp.where(inside, column + (sources[i] - i) * per, target_row)
    onehot = (lax.broadcasted_iota(jnp.int32, (slots, slots), 0) == target_row)
    ham[...] = jnp.where(onehot, jnp.float32(1.0), jnp.float32(0.0)).astype(jnp.bfloat16)
    for copy in k_copies:
        copy.wait()
    for band in range(bands):
        kp[band_slice(band), :] = jnp.dot(
            flat(land_k, band).astype(jnp.bfloat16), ham[...], preferred_element_type=jnp.float32
        ).astype(jnp.bfloat16)

    coef_live = lax.broadcasted_iota(jnp.int32, (rows, coef), 1) < coef_ref[0, 0]
    rank = lax.broadcasted_iota(jnp.int32, (rows, coef), 0)

    def live_mask(band):
        live = None
        for t in range(group):
            count = live_ref[0, sources[band * group + t]]
            inside = (rank >= t * per) & (rank < t * per + jnp.minimum(count, per))
            live = inside if live is None else live | inside
        return live & coef_live

    low[...] = jnp.zeros_like(low)
    contract = (((1,), (1,)), ((), ()))
    tile_sends = []
    for band in range(bands):
        for i in range(band * group, (band + 1) * group):
            if i == 0:
                own[0].wait()
                own[1].wait()
                continue
            for src, dst, ss, rs in ((f_hbm, land_f, f_send, f_recv), (a_hbm, land_a, a_send, a_recv)):
                pltpu.make_async_remote_copy(
                    src_ref=src.at[0], dst_ref=dst.at[i], send_sem=ss.at[0], recv_sem=rs.at[i],
                    device_id={"dev": sources[i]}, device_id_type=MESH,
                ).wait_recv()
        mask = live_mask(band)
        f_new = jnp.where(mask, flat(land_f, band), jnp.float32(0.0)).astype(jnp.bfloat16)
        a_new = jnp.where(mask, flat(land_a, band), jnp.float32(0.0)).astype(jnp.bfloat16)
        fm[band_slice(band), :] = f_new
        am[band_slice(band), :] = a_new
        upto = (band + 1) * rows
        tile = lax.dot_general(f_new, am[0:upto, :], contract, preferred_element_type=jnp.float32)
        tile += lax.dot_general(a_new, fm[0:upto, :], contract, preferred_element_type=jnp.float32)
        low[band_slice(band), 0:upto] = 0.5 * tile
        width = -(-upto // 128) * 128
        s_loc[band, :, 0:width] = low[band_slice(band), 0:width].astype(jnp.bfloat16)
        for r in range(1, n_grp):
            copy = pltpu.make_async_remote_copy(
                src_ref=s_loc.at[band, :, 0:width], dst_ref=s_in.at[r - 1, band, :, 0:width],
                send_sem=s_send.at[r - 1, band], recv_sem=s_recv.at[r - 1, band],
                device_id={"grp": (grp + r) % n_grp}, device_id_type=MESH,
            )
            copy.start()
            tile_sends.append(copy)

    for band in range(bands):
        ka[band_slice(band), :] = jnp.dot(
            kp[band_slice(band), :], am[...], preferred_element_type=jnp.float32
        )

    number = 0
    for band in range(bands):
        width = -(-((band + 1) * rows) // 128) * 128
        total = s_loc[band, :, 0:width].astype(jnp.float32)
        for r in range(1, n_grp):
            tile_sends[number].wait_recv()
            number += 1
            total += s_in[r - 1, band, :, 0:width].astype(jnp.float32)
        low[band_slice(band), 0:width] = total / coef
    lower = low[...]
    row_band = lax.broadcasted_iota(jnp.int32, (slots, slots), 0) // rows
    column_band = lax.broadcasted_iota(jnp.int32, (slots, slots), 1) // rows
    ham[...] = jnp.where(row_band >= column_band, lower, lower.T).astype(jnp.bfloat16)

    returns = []
    for band in reversed(range(bands)):
        mult = jnp.dot(
            kp[band_slice(band), :], ham[...], preferred_element_type=jnp.float32
        ).astype(jnp.bfloat16)
        grad = ka[band_slice(band), :] - jnp.dot(mult, fm[...], preferred_element_type=jnp.float32)
        grad = jnp.where(live_mask(band), grad, jnp.float32(0.0))
        for t in reversed(range(group)):
            i = band * group + t
            g_buf[i] = grad[t * per:(t + 1) * per, :].astype(jnp.bfloat16)
            if i == 0:
                copy = pltpu.make_async_copy(g_buf.at[0], out_ref.at[dev], own_sem.at[0])
            else:
                copy = pltpu.make_async_remote_copy(
                    src_ref=g_buf.at[i], dst_ref=out_ref.at[dev],
                    send_sem=g_send.at[i], recv_sem=g_recv.at[dev],
                    device_id={"dev": sources[i]}, device_id_type=MESH,
                )
                returns.append(copy)
            copy.start()
            if i == 0:
                last_own = copy

    for copy in outgoing + tile_sends + returns:
        copy.wait_send()
    last_own.wait()
    for i in range(1, n_dev):
        pltpu.make_async_remote_copy(
            src_ref=g_buf.at[i], dst_ref=out_ref.at[sources[i]],
            send_sem=g_send.at[i], recv_sem=g_recv.at[sources[i]],
            device_id={"dev": sources[i]}, device_id_type=MESH,
        ).wait_recv()


def shards(n_grp, n_dev, functions, applied, kernel, live_counts, coef_counts):
    slots, coef = functions.shape
    per = slots // n_dev
    bands = min(BANDS, n_dev)
    rows = slots // bands
    pieces = (n_dev, per, coef)
    bf16, f32 = jnp.bfloat16, jnp.float32
    dma = pltpu.SemaphoreType.DMA
    anywhere = pl.BlockSpec(memory_space=pl.ANY)
    scalars = pl.BlockSpec(memory_space=pltpu.SMEM)
    result = pl.pallas_call(
        functools.partial(body, n_grp, n_dev),
        out_shape=jax.ShapeDtypeStruct(pieces, bf16),
        in_specs=[scalars, scalars, anywhere, anywhere, anywhere],
        out_specs=anywhere,
        scratch_shapes=[
            pltpu.VMEM(pieces, bf16), pltpu.VMEM(pieces, bf16), pltpu.VMEM((n_dev, per, slots), bf16),
            pltpu.VMEM((slots, coef), bf16), pltpu.VMEM((slots, coef), bf16),
            pltpu.VMEM((slots, slots), bf16), pltpu.VMEM((slots, coef), f32),
            pltpu.VMEM((bands, rows, slots), bf16), pltpu.VMEM((n_grp - 1, bands, rows, slots), bf16),
            pltpu.VMEM((slots, slots), f32), pltpu.VMEM((slots, slots), bf16),
            pltpu.VMEM(pieces, bf16),
            dma((n_dev,)), dma((n_dev,)), dma((n_dev,)), dma((n_dev,)),
            dma((n_grp - 1, bands)), dma((n_grp - 1, bands)),
            dma((n_dev,)), dma((n_dev,)), dma((n_dev,)), dma((2,)),
        ],
        compiler_params=pltpu.CompilerParams(
            collective_id=0, has_side_effects=True, vmem_limit_bytes=60 * 1024 * 1024
        ),
        name="region_step",
    )(
        live_counts, coef_counts, functions.reshape(pieces), applied.reshape(pieces),
        kernel.reshape(n_dev, per, slots),
    )
    return result.reshape(slots, coef)


def solution(mesh):
    placed = (P("dev", "grp"), P("dev", "grp"), P("dev", None), P("dev", None), P("grp", "dev"))
    return jax.shard_map(
        functools.partial(shards, mesh.shape["grp"], mesh.shape["dev"]),
        mesh=mesh, in_specs=placed, out_specs=P("dev", "grp"), check_vma=False,
    )
```

time: 186 us -> 104 us (0.56); the launches traced: 183 us -> 103 us
  Pallas kernels: 0 us -> 100 us
  waiting for transfers between devices: 83 us -> 0 us
  blocking collectives: 65.3 us -> 0 us
  between operations: 14.1 us -> 0.66 us
  matrix products: 7.28 us -> 0 us
  starting transfers between devices: 5.94 us -> 0 us
  other arithmetic: 3.72 us -> 0 us
    pallas_call x0 -> x1, Pallas kernels: none -> 100 us  [shards(): pl.pallas_call(functools.partial(body, n_grp, n_dev), out_shape=jax.Shape...]
    all_to_all x2 -> x0, blocking collectives: 65.3 us -> none  [the longest x1 32.8 us: shards(): lax.all_to_all(functions, 'dev', split_axis=0, concat_axis=0, tiled=True)]
    reduce_scatter x1 -> x0, waiting for transfers between devices: 30.3 us -> none  [shards(): lax.psum_scatter(symmetric.astype(jnp.bfloat16), 'grp', scatter_dimension...]
    all_gather x1 -> x0, waiting for transfers between devices: 27.7 us -> none  [shards(): lax.all_gather(columns, 'grp', axis=1, tiled=True)]
    all_to_all x1 -> x0, waiting for transfers between devices: 25 us -> none  [shards(): lax.all_to_all(applied, 'dev', split_axis=0, concat_axis=0, tiled=True)]
    dot_general x4 -> x0, matrix products: 7.28 us -> none  [the longest x1 2.58 us: shards(): jnp.dot(lax.all_gather(columns, 'grp', axis=1, tiled=True), masked_funcs,...]
    all_to_all x1 -> x0, starting transfers between devices: 5.9 us -> none  [shards(): lax.all_to_all(applied, 'dev', split_axis=0, concat_axis=0, tiled=True)]
    convert_element_type x1 -> x0, other arithmetic: 2.99 us -> none  [shards(): symmetric.astype(jnp.bfloat16)]
  transfers between devices with their start and end apart: 3 -> 0, of which waited for: 3 -> 0; matrix products, arithmetic and copies ran while one was open for 0% -> 0% of each run, Pallas kernels for 0% -> 0%
where the time goes in v1:
time: 104 us; the launch traced here: 103 us
  Pallas kernels  100 us (96%)
  local copies, waits for them, and re-layouts  2.36 us (2%)
    pallas_call x1, Pallas kernels, shards(): pl.pallas_call(functools.partial(body, n_grp, n_dev), out_shape=jax.Shape...  100 us
    unnamed x1, local copies, waits for them, and re-layouts  2.36 us

profile of v1, /device:TPU:9, one launch (start us, length us, event | category | flops | bytes accessed | tf_op | source)
XLA Modules:
  0.0 103.3 jit_solution(7002688582918126038)
XLA Ops:
  0.7 100.3 %region_step.1 = bf16[8,96,768]{2,1,0:T(8,128)(2,1)} custom-call(s32[1,8]{1,0:T(1,128)} %live_ref.1, s32[1,1]{1,0:T(1,128)S(6)} %copy.7.coef_ref, bf16[8,96,768]{2,1,0:T(8,128)(2,1)} %bitcast.5, bf16[8,96,768]{2,1,0:T(8,128)(2,1)} %bitcast.6, bf16[8,96,768]{2,1,0:T(8,128)(2,1)} %bitcast.7), custom_call_target="tpu_custom_call" | custom-call | tf_op jit(solution)/shard_map/region_step/pallas_call | solution.py:215
  101.0 2.4 %copy.8 = bf16[768,768]{1,0:T(8,128)(2,1)} copy(bf16[768,768]{1,0:T(8,128)(2,1)} %bitcast.4) | data formatting | bytes 2359296

commit v2 on v1

--- a/solution.py
+++ b/solution.py
@@ -117,8 +117,36 @@
 
     low[...] = jnp.zeros_like(low)
     contract = (((1,), (1,)), ((), ()))
-    tile_sends = []
-    for band in range(bands):
+    steps = n_grp.bit_length() - 1
+    half_rows = rows // 2
+
+    def width_of(band):
+        return -(-((band + 1) * rows) // 128) * 128
+
+    def tile_copy(step, band, half):
+        bit = 2 ** (step if half == 0 else steps - 1 - step)
+        peer = grp + bit * (1 - 2 * ((grp // bit) % 2))
+        place = (step, band, pl.ds(half * half_rows, half_rows), pl.ds(0, width_of(band)))
+        return pltpu.make_async_remote_copy(
+            src_ref=s_loc.at[place], dst_ref=s_in.at[place],
+            send_sem=s_send.at[step, band, half], recv_sem=s_recv.at[step, band, half],
+            device_id={"grp": peer}, device_id_type=MESH,
+        )
+
+    def advance(step, band):
+        wide = pl.ds(0, width_of(band))
+        for half in range(2):
+            here = pl.ds(half * half_rows, half_rows)
+            tile_copy(step, band, half).wait_recv()
+            total = s_loc[step, band, here, wide].astype(jnp.float32)
+            total += s_in[step, band, here, wide].astype(jnp.float32)
+            if step + 1 < steps:
+                s_loc[step + 1, band, here, wide] = total.astype(jnp.bfloat16)
+                tile_copy(step + 1, band, half).start()
+            else:
+                low[pl.ds(band * rows + half * half_rows, half_rows), wide] = total / coef
+
+    def arrive(band):
         for i in range(band * group, (band + 1) * group):
             if i == 0:
                 own[0].wait()
@@ -138,35 +166,38 @@
         tile = lax.dot_general(f_new, am[0:upto, :], contract, preferred_element_type=jnp.float32)
         tile += lax.dot_general(a_new, fm[0:upto, :], contract, preferred_element_type=jnp.float32)
         low[band_slice(band), 0:upto] = 0.5 * tile
-        width = -(-upto // 128) * 128
-        s_loc[band, :, 0:width] = low[band_slice(band), 0:width].astype(jnp.bfloat16)
-        for r in range(1, n_grp):
-            copy = pltpu.make_async_remote_copy(
-                src_ref=s_loc.at[band, :, 0:width], dst_ref=s_in.at[r - 1, band, :, 0:width],
-                send_sem=s_send.at[r - 1, band], recv_sem=s_recv.at[r - 1, band],
-                device_id={"grp": (grp + r) % n_grp}, device_id_type=MESH,
+        wide = pl.ds(0, width_of(band))
+        s_loc[0, band, :, wide] = low[band_slice(band), wide].astype(jnp.bfloat16)
+        for half in range(2):
+            tile_copy(0, band, half).start()
+
+    def multiply_kernel(first, last):
+        for band in range(first, last):
+            ka[band_slice(band), :] = jnp.dot(
+                kp[band_slice(band), :], am[...], preferred_element_type=jnp.float32
             )
-            copy.start()
-            tile_sends.append(copy)
-
-    for band in range(bands):
-        ka[band_slice(band), :] = jnp.dot(
-            kp[band_slice(band), :], am[...], preferred_element_type=jnp.float32
-        )
-
-    number = 0
-    for band in range(bands):
-        width = -(-((band + 1) * rows) // 128) * 128
-        total = s_loc[band, :, 0:width].astype(jnp.float32)
-        for r in range(1, n_grp):
-            tile_sends[number].wait_recv()
-            number += 1
-            total += s_in[r - 1, band, :, 0:width].astype(jnp.float32)
-        low[band_slice(band), 0:width] = total / coef
-    lower = low[...]
-    row_band = lax.broadcasted_iota(jnp.int32, (slots, slots), 0) // rows
-    column_band = lax.broadcasted_iota(jnp.int32, (slots, slots), 1) // rows
-    ham[...] = jnp.where(row_band >= column_band, lower, lower.T).astype(jnp.bfloat16)
+
+    def mirror(start, size):
+        lower = low[:, start:start + size]
+        upper = low[start:start + size, :].T
+        row_band = lax.broadcasted_iota(jnp.int32, (slots, size), 0) // rows
+        column_band = (lax.broadcasted_iota(jnp.int32, (slots, size), 1) + start) // rows
+        ham[:, start:start + size] = jnp.where(row_band >= column_band, lower, upper).astype(jnp.bfloat16)
+
+    for turn in range(bands + steps):
+        if turn < bands:
+            arrive(turn)
+        for step in range(steps):
+            if 0 <= turn - 1 - step < bands:
+                advance(step, turn - 1 - step)
+        if turn == bands - 1:
+            multiply_kernel(0, bands // 2)
+        if turn == bands + steps - 2:
+            mirror(0, slots)
+            multiply_kernel(bands // 2, bands)
+    edge = (slots - rows) // 128 * 128
+    ham[band_slice(bands - 1), :] = low[band_slice(bands - 1), :].astype(jnp.bfloat16)
+    mirror(edge, slots - edge)
 
     returns = []
     for band in reversed(range(bands)):
@@ -191,6 +222,9 @@
             if i == 0:
                 last_own = copy
 
+    tile_sends = [
+        tile_copy(step, band, half) for step in range(steps) for band in range(bands) for half in range(2)
+    ]
     for copy in outgoing + tile_sends + returns:
         copy.wait_send()
     last_own.wait()
@@ -208,6 +242,7 @@
     bands = min(BANDS, n_dev)
     rows = slots // bands
     pieces = (n_dev, per, coef)
+    steps = n_grp.bit_length() - 1
     bf16, f32 = jnp.bfloat16, jnp.float32
     dma = pltpu.SemaphoreType.DMA
     anywhere = pl.BlockSpec(memory_space=pl.ANY)
@@ -221,11 +256,11 @@
             pltpu.VMEM(pieces, bf16), pltpu.VMEM(pieces, bf16), pltpu.VMEM((n_dev, per, slots), bf16),
             pltpu.VMEM((slots, coef), bf16), pltpu.VMEM((slots, coef), bf16),
             pltpu.VMEM((slots, slots), bf16), pltpu.VMEM((slots, coef), f32),
-            pltpu.VMEM((bands, rows, slots), bf16), pltpu.VMEM((n_grp - 1, bands, rows, slots), bf16),
+            pltpu.VMEM((steps, bands, rows, slots), bf16), pltpu.VMEM((steps, bands, rows, slots), bf16),
             pltpu.VMEM((slots, slots), f32), pltpu.VMEM((slots, slots), bf16),
             pltpu.VMEM(pieces, bf16),
             dma((n_dev,)), dma((n_dev,)), dma((n_dev,)), dma((n_dev,)),
-            dma((n_grp - 1, bands)), dma((n_grp - 1, bands)),
+            dma((steps, bands, 2)), dma((steps, bands, 2)),
             dma((n_dev,)), dma((n_dev,)), dma((n_dev,)), dma((2,)),
         ],
         compiler_params=pltpu.CompilerParams(

time: 104 us -> 96.6 us (0.929)
  Pallas kernels: 100 us -> 92.7 us
    pallas_call x1, Pallas kernels: 100 us -> 92.7 us  [shards(): pl.pallas_call(functools.partial(body, n_grp, n_dev), out_shape=jax.Shape...]
where the time goes in v2:
time: 96.6 us; the launch traced here: 95.7 us
  Pallas kernels  92.7 us (96%)
  local copies, waits for them, and re-layouts  2.36 us (2%)
    pallas_call x1, Pallas kernels, shards(): pl.pallas_call(functools.partial(body, n_grp, n_dev), out_shape=jax.Shape...  92.7 us
    unnamed x1, local copies, waits for them, and re-layouts  2.36 us

profile of v2, /device:TPU:9, one launch (start us, length us, event | category | flops | bytes accessed | tf_op | source)
XLA Modules:
  0.0 95.7 jit_solution(3912854902506551978)
XLA Ops:
  0.7 92.7 %region_step.1 = bf16[8,96,768]{2,1,0:T(8,128)(2,1)} custom-call(s32[1,8]{1,0:T(1,128)} %live_ref.1, s32[1,1]{1,0:T(1,128)S(6)} %copy.7.coef_ref, bf16[8,96,768]{2,1,0:T(8,128)(2,1)} %bitcast.5, bf16[8,96,768]{2,1,0:T(8,128)(2,1)} %bitcast.6, bf16[8,96,768]{2,1,0:T(8,128)(2,1)} %bitcast.7), custom_call_target="tpu_custom_call" | custom-call | tf_op jit(solution)/shard_map/region_step/pallas_call | solution.py:250
  93.4 2.4 %copy.8 = bf16[768,768]{1,0:T(8,128)(2,1)} copy(bf16[768,768]{1,0:T(8,128)(2,1)} %bitcast.4) | data formatting | bytes 2359296

commit v3 on v2

--- a/solution.py
+++ b/solution.py
@@ -15,7 +15,7 @@
 def arrival_orders(chips):
     half = chips // 2
     return [
-        sorted(range(chips), key=lambda s: (abs(s - z), (s < half) != (z < half), s)) for z in range(chips)
+        sorted(range(chips), key=lambda s: (s != z, -abs(s - z), (s < half) != (z < half), s)) for z in range(chips)
     ]
 
 
@@ -200,13 +200,14 @@
     mirror(edge, slots - edge)
 
     returns = []
-    for band in reversed(range(bands)):
+    own_bands = -(-CORES // group)
+    for band in [*range(own_bands, bands), *reversed(range(own_bands))]:
         mult = jnp.dot(
             kp[band_slice(band), :], ham[...], preferred_element_type=jnp.float32
         ).astype(jnp.bfloat16)
         grad = ka[band_slice(band), :] - jnp.dot(mult, fm[...], preferred_element_type=jnp.float32)
         grad = jnp.where(live_mask(band), grad, jnp.float32(0.0))
-        for t in reversed(range(group)):
+        for t in range(group):
             i = band * group + t
             g_buf[i] = grad[t * per:(t + 1) * per, :].astype(jnp.bfloat16)
             if i == 0:

time: 96.6 us -> 90.6 us (0.938)
  Pallas kernels: 92.7 us -> 87.4 us
    pallas_call x1, Pallas kernels: 92.7 us -> 87.4 us  [shards(): pl.pallas_call(functools.partial(body, n_grp, n_dev), out_shape=jax.Shape...]
where the time goes in v3:
time: 90.6 us; the launch traced here: 90.4 us
  Pallas kernels  87.4 us (96%)
  local copies, waits for them, and re-layouts  2.36 us (3%)
    pallas_call x1, Pallas kernels, shards(): pl.pallas_call(functools.partial(body, n_grp, n_dev), out_shape=jax.Shape...  87.4 us
    unnamed x1, local copies, waits for them, and re-layouts  2.36 us

profile of v3, /device:TPU:9, one launch (start us, length us, event | category | flops | bytes accessed | tf_op | source)
XLA Modules:
  0.0 90.4 jit_solution(17169574004275274995)
XLA Ops:
  0.7 87.4 %region_step.1 = bf16[8,96,768]{2,1,0:T(8,128)(2,1)} custom-call(s32[1,8]{1,0:T(1,128)} %live_ref.1, s32[1,1]{1,0:T(1,128)S(6)} %copy.7.coef_ref, bf16[8,96,768]{2,1,0:T(8,128)(2,1)} %bitcast.5, bf16[8,96,768]{2,1,0:T(8,128)(2,1)} %bitcast.6, bf16[8,96,768]{2,1,0:T(8,128)(2,1)} %bitcast.7), custom_call_target="tpu_custom_call" | custom-call | tf_op jit(solution)/shard_map/region_step/pallas_call | solution.py:251
  88.0 2.4 %copy.8 = bf16[768,768]{1,0:T(8,128)(2,1)} copy(bf16[768,768]{1,0:T(8,128)(2,1)} %bitcast.4) | data formatting | bytes 2359296
